TPU v7x, 32 devices: a whole 2x2x4 slice. The times are simulated.
32 devices in a mesh: seq: 8 (over y, x, core), seg: 4 (over z).
Axes of the slice: x: 2, y: 2, z: 4, core: 2. Of those that a mesh axis runs over, the one named last changes fastest.
Arguments:
- query_rows: bfloat16 [4, 2048, 4, 128], P('seg', 'seq'), may hold values from -6 to 6
- key_rows: bfloat16 [4, 2048, 2, 4, 128], P('seg', 'seq'), may hold values from -6 to 6
- value_rows: bfloat16 [4, 2048, 2, 4, 128], P('seg', 'seq'), may hold values from -6 to 6
- out_gain: float32 [4, 128], replicated, may hold values from 0.5 to 1.5
- initial_state: float32 [4, 128, 128], replicated, may hold values from -24 to 24
Outputs:
- normed_out: bfloat16 [4, 2048, 4, 128], P('seg', 'seq')
All inputs are finite; a program needn't handle non-finite values.
Results may differ from a plain program's by a relative error of at most 0.004.
Values sent between devices are 32-bit elements; how exact they have to be, the bound alone decides.
A program may use at most 128 MiB of HBM per device.

v0:
```python
import jax
import jax.numpy as jnp
from jax import lax
from jax.sharding import PartitionSpec as P

DK = 128
DV = 128
HEADS = 4
REFL = 2
GROUP = 128


highest = lax.Precision.HIGHEST


def carried_in(part, axis, combine, identity):
    place = lax.axis_index(axis)
    gathered = lax.all_gather(part, axis)
    state = jnp.zeros_like(part) + jnp.asarray(identity, part.dtype)

    def one(step, state):
        return combine(state, lax.dynamic_index_in_dim(gathered, step, 0, False))

    return lax.fori_loop(0, place, one, state)


def unit_keys(raw):
    raw = raw.astype(jnp.float32)
    return raw * lax.rsqrt(jnp.sum(raw * raw, axis=-1, keepdims=True) + 1e-06)


def solve_single(matrix, target):
    return jax.scipy.linalg.solve_triangular(matrix, target, lower=True, unit_diagonal=True)


def block_factors(query, keyed, valued):
    steps = keyed.shape[-2]
    tokens = query.shape[-2]
    key_gram = jnp.einsum("...id,...jd->...ij", keyed, keyed, precision=highest)
    lower_unit = jnp.eye(steps, dtype=jnp.float32) + jnp.tril(2.0 * key_gram, -1)
    target = jnp.concatenate([2.0 * keyed, 2.0 * valued], axis=-1)
    flat_lower = lower_unit.reshape(-1, steps, steps)
    flat_target = target.reshape(-1, steps, target.shape[-1])
    solved = jax.vmap(solve_single)(flat_lower, flat_target).reshape(target.shape)
    weights = solved[..., : keyed.shape[-1]]
    updates = solved[..., keyed.shape[-1] :]
    visible = jnp.arange(steps)[None, :] <= REFL * jnp.arange(tokens)[:, None] + (REFL - 1)
    scores = jnp.where(
        visible, jnp.einsum("...td,...ld->...tl", query, keyed, precision=highest), 0.0
    )
    return (weights, updates, scores)


def compose(first_pair, second_pair):
    second_trans = second_pair[..., :DK]
    moved = jnp.einsum("...de,...ef->...df", second_trans, first_pair, precision=highest)
    added = jnp.concatenate([jnp.zeros_like(second_trans), second_pair[..., DK:]], axis=-1)
    return moved + added


def identity_pair():
    eye_part = jnp.broadcast_to(jnp.eye(DK, dtype=jnp.float32), (HEADS, DK, DK))
    return jnp.concatenate([eye_part, jnp.zeros((HEADS, DK, DV), jnp.float32)], axis=-1)


def apply_pair(pair, state):
    return jnp.einsum("hde,hef->hdf", pair[..., :DK], state, precision=highest) + pair[..., DK:]


def ordered_prefix(stacked, position):

    def ordered_accumulate(carry, piece):
        return (compose(carry, piece), carry)

    closing, before_all = lax.scan(ordered_accumulate, identity_pair(), stacked)
    return (lax.dynamic_index_in_dim(before_all, position, 0, keepdims=False), closing)


def per_device(query_rows, key_rows, value_rows, out_gain, initial_state):
    tokens = query_rows.shape[1]
    nblock = tokens // GROUP
    query = (
        query_rows[0].astype(jnp.float32).reshape(nblock, GROUP, HEADS, DK).transpose(0, 2, 1, 3)
    )
    keyed = unit_keys(key_rows[0]).reshape(nblock, GROUP * REFL, HEADS, DK).transpose(0, 2, 1, 3)
    valued = (
        value_rows[0]
        .astype(jnp.float32)
        .reshape(nblock, GROUP * REFL, HEADS, DV)
        .transpose(0, 2, 1, 3)
    )
    weights, updates, scores = block_factors(query, keyed, valued)
    trans_block = jnp.eye(DK, dtype=jnp.float32) - jnp.einsum(
        "chld,chle->chde", keyed, weights, precision=highest
    )
    state_block = jnp.einsum("chld,chle->chde", keyed, updates, precision=highest)
    block_pairs = jnp.concatenate([trans_block, state_block], axis=-1)
    project = query - jnp.einsum("chtl,chld->chtd", scores, weights, precision=highest)
    local_read = jnp.einsum("chtl,chle->chte", scores, updates, precision=highest)

    def body_accumulate(carry, piece):
        return (compose(carry, piece), carry)

    own_pair, before = lax.scan(body_accumulate, identity_pair(), block_pairs)
    reach = jnp.einsum("chtd,chde->chte", project, before[..., :DK], precision=highest)
    base_read = (
        jnp.einsum("chtd,chde->chte", project, before[..., DK:], precision=highest) + local_read
    )
    stacked = lax.all_gather(own_pair[None], "seq", axis=0, tiled=True)
    seq_before, seg_total = ordered_prefix(stacked, lax.axis_index("seq"))
    seg_before = carried_in(seg_total, "seg", compose, identity_pair())
    entry_state = apply_pair(seg_before, initial_state)
    incoming = apply_pair(seq_before, entry_state)
    reads = jnp.einsum("chtd,hde->chte", reach, incoming, precision=highest) + base_read
    reads = reads.transpose(0, 2, 1, 3).reshape(1, tokens, HEADS, DV)
    scale = lax.rsqrt(jnp.mean(reads * reads, axis=-1, keepdims=True) + 1e-06)
    return (reads * scale * out_gain).astype(jnp.bfloat16)


def solution(mesh):
    return jax.shard_map(
        per_device,
        mesh=mesh,
        in_specs=(
            P("seg", "seq", None, None),
            P("seg", "seq", None, None, None),
            P("seg", "seq", None, None, None),
            P(),
            P(),
        ),
        out_specs=P("seg", "seq", None, None),
        check_vma=False,
    )
```

profile of v0, /device:TPU:29, one launch (start us, length us, event | category | flops | bytes accessed | tf_op | source)
XLA Modules:
  0.0 318.5 jit_solution(12129353922683288932)
XLA Ops:
  7.4 1.8 multiply_reduce_fusion
  11.0 1.3 bitcast_multiply_fusion
  12.3 2.3 select_add_fusion
  15.0 5.8 %while.38 = (s32[]{:T(128)}, f32[8,256,256]{2,1,0:T(8,128)S(1)}, s32[2,2]{1,0:T(2,128)S(1)}, f32[2,8,128,128]{3,2,0,1:T(8,128)}, s32[]{:T(128)}) while((s32[]{:T(128)}, f32[8,256,256]{2,1,0:T(8,128)S(1)}, s32[2,2]{1,0:T(2,128)S(1)}, f32[2,8,128,128]{3,2,0,1:T(8,128)}, s32[]{:T(128)}) %tuple.63), condition=%wide.while_cond, body=%wide.while_body.sunk | while | flops 2 | bytes 1049709 | solution.py:33
  15.7 2.2 bitcast_dynamic-update-slice_fusion.8
  18.5 2.2 bitcast_dynamic-update-slice_fusion.8
  20.8 158.6 %custom-call.4 = f32[8,2,128,128]{2,3,1,0:T(8,128)} custom-call(f32[8,2,128,128]{3,2,1,0:T(8,128)} %bitcast.120), custom_call_target="InvertDiagBlocksLowerTriangular" | custom-call | tf_op jit(solution)/shard_map/vmap(jit(_solve_triangular))/triangular_solve | solution.py:33
  179.4 1.8 pad_maximum_fusion
  181.3 1.1 fusion.8
  183.4 1.1 fusion.22
  184.7 2.2 convolution_subtract_fusion.2
  186.9 2.2 fusion.13
  191.0 9.2 %while.35 = (s32[]{:T(128)}, f32[4,128,256]{2,1,0:T(8,128)}, f32[2,4,128,256]{3,2,1,0:T(8,128)}, f32[2,4,128,256]{2,3,1,0:T(8,128)}, s32[]{:T(128)}) while((s32[]{:T(128)}, f32[4,128,256]{2,1,0:T(8,128)}, f32[2,4,128,256]{3,2,1,0:T(8,128)}, f32[2,4,128,256]{2,3,1,0:T(8,128)}, s32[]{:T(128)}) %tuple.66), condition=%wide.region_2.3_spmd, body=%wide.region_1.2_spmd.sunk | while | flops 201457664 | bytes 6291533 | solution.py:104
  194.2 1.4 convolution_add_fusion.9
  198.8 1.4 convolution_add_fusion.9
  200.3 37.8 %all-gather.5.cloned.1.call-done = f32[32,128,256]{2,1,0:T(8,128)} async-done(((f32[4,128,256]{2,1,0:T(8,128)}), f32[32,128,256]{2,1,0:T(8,128)}) %all-gather.5.cloned.1.call-update) | async-done | bytes 4194320 | tf_op jit(solution)/shard_map/all_gather | solution.py:109
  238.1 21.0 %while.36 = (s32[]{:T(128)}, f32[4,128,256]{2,1,0:T(8,128)S(1)}, f32[8,4,128,256]{3,2,1,0:T(8,128)}, f32[8,4,128,256]{3,2,1,0:T(8,128)}, s32[]{:T(128)}) while((s32[]{:T(128)}, f32[4,128,256]{2,1,0:T(8,128)S(1)}, f32[8,4,128,256]{3,2,1,0:T(8,128)}, f32[8,4,128,256]{3,2,1,0:T(8,128)}, s32[]{:T(128)}) %tuple.80), condition=%wide.region_4.5_spmd, body=%wide.region_3.4_spmd.sunk | while | flops 201457664 | bytes 5242957 | solution.py:75
  238.2 1.1 dynamic-slice_bitcast_fusion.5
  240.8 1.1 dynamic-slice_bitcast_fusion.5
  243.4 1.1 dynamic-slice_bitcast_fusion.5
  246.1 1.1 dynamic-slice_bitcast_fusion.5
  248.7 1.1 dynamic-slice_bitcast_fusion.5
  251.3 1.1 dynamic-slice_bitcast_fusion.5
  256.5 1.1 dynamic-slice_bitcast_fusion.5
  261.6 2.8 convolution_subtract_fusion.1
  265.7 1.9 fusion.5
  267.6 1.1 dynamic-slice_bitcast_fusion.2
  268.7 34.8 %all-gather.7.cloned.1.call-done = f32[16,128,256]{2,1,0:T(8,128)} async-done(((f32[4,128,256]{2,1,0:T(8,128)}), f32[16,128,256]{2,1,0:T(8,128)}) %all-gather.7.cloned.1.call-update) | async-done | bytes 2097168 | tf_op jit(solution)/shard_map/all_gather | solution.py:18
  303.5 5.3 %while.37 = (s32[]{:T(128)}, f32[4,128,256]{2,1,0:T(8,128)S(1)}, s32[]{:T(128)}, f32[4,4,128,256]{3,2,1,0:T(8,128)}, s32[]{:T(128)}, /*index=5*/s32[]{:T(128)}, s32[]{:T(128)}) while((s32[]{:T(128)}, f32[4,128,256]{2,1,0:T(8,128)S(1)}, s32[]{:T(128)}, f32[4,4,128,256]{3,2,1,0:T(8,128)}, s32[]{:T(128)}, /*index=5*/s32[]{:T(128)}, ...), condition=%wide.region_6.7_spmd, body=%wide.region_5.6_spmd.sunk | while | flops 201457664 | bytes 4194427 | solution.py:24
  305.3 1.1 dynamic-slice_bitcast_fusion.6
  307.1 1.1 dynamic-slice_bitcast_fusion.6
  310.5 1.1 fusion.26
  (116 shorter events, 35.2 us)
Async XLA Ops:
  6.5 302.2 %copy-start = (f32[4,128,128]{2,1,0:T(8,128)S(1)}, f32[4,128,128]{2,1,0:T(8,128)}, u32[]{:S(2)}) copy-start(f32[4,128,128]{2,1,0:T(8,128)} %param.15) | copy-start | bytes 786436
  6.5 3.1 copy-start.4
  6.5 3.2 copy-start.9
  6.5 231.6 %all-gather.5.cloned.1.call-start = ((), (), s32[]{:S(2)}) async-start(), calls=%async_computation | async-start | bytes 4718592 | tf_op jit(solution)/shard_map/all_gather | solution.py:109
  12.3 2.3 copy-start.7
  179.4 1.9 copy-start.6
  184.7 4.4 %copy-start.2 = (f32[8,256,256]{2,1,0:T(8,128)}, f32[8,256,256]{2,1,0:T(8,128)S(1)}, u32[]{:S(2)}) copy-start(f32[8,256,256]{2,1,0:T(8,128)S(1)} %pad_maximum_fusion.1) | copy-start | bytes 6291460
  200.2 103.2 %all-gather.7.cloned.1.call-start = ((), (), s32[]{:S(2)}) async-start(), calls=%async_computation.1 | async-start | bytes 2621440 | tf_op jit(solution)/shard_map/all_gather | solution.py:18
  238.1 21.9 %copy-start.8 = (bf16[1,256,4,128]{3,2,1,0:T(4,128)(2,1)S(1)}, bf16[1,256,4,128]{3,2,1,0:T(4,128)(2,1)}, u32[]{:S(2)}) copy-start(bf16[1,256,4,128]{3,2,1,0:T(4,128)(2,1)} %param.11) | copy-start | bytes 786436
  259.1 0.8 copy-start.1
  260.0 1.6 copy-start.3
  260.0 4.3 %copy-start.5 = (f32[2,4,128,256]{3,2,1,0:T(8,128)S(1)}, f32[2,4,128,256]{3,2,1,0:T(8,128)}, u32[]{:S(2)}) copy-start(f32[2,4,128,256]{3,2,1,0:T(8,128)} %get-tuple-element.78) | copy-start | bytes 3145732
  308.8 1.7 copy-start.10
Sparse Core Ops, SparseCore 0:
  200.4 37.7 all-gather.4
  260.1 43.3 all-gather.6
where the time goes:
time: 320 us; the launch traced here: 319 us
  other arithmetic  168 us (52%)
  waiting for transfers between devices  72.6 us (23%)
  local copies, waits for them, and re-layouts  36.5 us (11%)
  matrix products  27.3 us (9%)
  between operations  13.8 us (4%)
    another operation x7, other arithmetic, solve_single(): jax.scipy.linalg.solve_triangular(matrix, target, lower=True, unit_diagon...  160 us
    all_gather x1, waiting for transfers between devices, per_device(): stacked = lax.all_gather(own_pair[None], 'seq', axis=0, tiled=True)  37.8 us
    all_gather x1, waiting for transfers between devices, carried_in(): gathered = lax.all_gather(part, axis)  34.8 us
    dot_general x13, matrix products, compose(): jnp.einsum('...de,...ef->...df', second_trans, first_pair, precision=high...  9.22 us
    squeeze x8, local copies, waits for them, and re-layouts, ordered_prefix(): closing, before_all = lax.scan(ordered_accumulate, identity_pair(), stacked)  8.7 us
    dynamic_update_slice x8, local copies, waits for them, and re-layouts, ordered_prefix(): closing, before_all = lax.scan(ordered_accumulate, identity_pair(), stacked)  6.85 us
  transfers between devices with their start and end apart: 2, of which 2 were waited for; matrix products, arithmetic and copies ran while one was open for 2% of the time, Pallas kernels for 0%

commit v1 on v0

v1 whole, which is shorter than its diff:
```python
import functools

import jax
import jax.numpy as jnp
from jax import lax
from jax.experimental import pallas as pl
from jax.experimental.pallas import tpu as pltpu
from jax.sharding import PartitionSpec as P

F32 = jnp.float32
BF16 = jnp.bfloat16
REFL = 2
BLK = 128
SUB = 16
MESH = pl.DeviceIdType.MESH


def dot(a, b):
    return lax.dot_general(a, b, (((1,), (0,)), ((), ())), preferred_element_type=F32)


def dot_bt(a, b):
    return lax.dot_general(a, b, (((1,), (1,)), ((), ())), preferred_element_type=F32)


def dot_at(a, b):
    return lax.dot_general(a, b, (((0,), (0,)), ((), ())), preferred_element_type=F32)


def split(x):
    high = x.astype(BF16)
    return high, (x - high.astype(F32)).astype(BF16)


def dot3(a, b):
    ah, al = a
    bh, bl = b
    return dot(ah, bh) + (dot(ah, bl) + dot(al, bh))


def iota(shape, axis):
    return lax.broadcasted_iota(jnp.int32, shape, axis)


def local_kernel(heads, q_ref, k_ref, v_ref, pair_ref, reach_ref, base_ref, dsc, nsc):
    steps = k_ref.shape[0]
    dk = q_ref.shape[1] // heads
    dv = v_ref.shape[1] // heads
    nblk = steps // BLK
    tok = BLK // REFL
    row, col = iota((BLK, BLK), 0), iota((BLK, BLK), 1)
    eye = row == col
    lane = iota((SUB, BLK), 1)
    chunks = [(h, c) for h in range(heads) for c in range(nblk)]
    count = len(chunks)

    keys, lowers, rcols, rrows = [], [], [], []
    for n, (h, c) in enumerate(chunks):
        key = k_ref[c * BLK : (c + 1) * BLK, h * dk : (h + 1) * dk]
        gram = dot_bt(key, key)
        diag = jnp.where(eye, gram, 0.0)
        rcol = lax.rsqrt(jnp.sum(diag, axis=1, keepdims=True) + 1e-6)
        rrow = lax.rsqrt(jnp.sum(diag, axis=0, keepdims=True) + 1e-6)
        lower = jnp.where(row > col, gram * (2.0 * rcol) * rrow, 0.0)
        packed = jnp.zeros((SUB, BLK), F32)
        for g in range(BLK // SUB):
            packed = jnp.where(lane // SUB == g, lower[g * SUB : (g + 1) * SUB], packed)
        dsc[n * SUB : (n + 1) * SUB, :] = packed
        keys.append(key)
        lowers.append(lower)
        rcols.append(rcol)
        rrows.append(rrow)

    lane_c = iota((count, BLK), 1)
    solved = []
    for i in range(SUB):
        line = dsc[pl.ds(i, count, stride=SUB), :]
        total = jnp.where(lane_c % SUB == i, 1.0, 0.0)
        for j in range(i):
            factor = jnp.take_along_axis(line, (lane_c // SUB) * SUB + j, axis=1)
            total = total - factor * solved[j]
        solved.append(total)
        nsc[pl.ds(i, count, stride=SUB), :] = total

    inverses = []
    for n in range(count):
        packed = nsc[n * SUB : (n + 1) * SUB, :]
        inverses.append(
            jnp.concatenate(
                [jnp.where(lane // SUB == g, packed, 0.0) for g in range(BLK // SUB)], axis=0
            )
        )
    size = SUB
    while size < BLK:
        mask = (row // size != col // size) & (row // (2 * size) == col // (2 * size))
        for n in range(count):
            inv = split(inverses[n])
            part = dot3(split(jnp.where(mask, lowers[n], 0.0)), inv)
            inverses[n] = inverses[n] - dot3(inv, split(part))
        size *= 2

    for h in range(heads):
        trans = add = None
        for c in range(nblk):
            n = h * nblk + c
            key, rcol, rrow = keys[n], rcols[n], rrows[n]
            value = v_ref[c * BLK : (c + 1) * BLK, h * dv : (h + 1) * dv]
            query = q_ref[c * tok : (c + 1) * tok, h * dk : (h + 1) * dk]
            nk = split(inverses[n] * (2.0 * rrow))
            nv = split(inverses[n] * 2.0)
            weights = dot(nk[0], key) + dot(nk[1], key)
            updates = dot(nv[0], value) + dot(nv[1], value)
            wu = jnp.concatenate([weights, updates], axis=1)
            scaled = split(wu * rcol)
            moved = dot_at(key, scaled[0]) + dot_at(key, scaled[1])
            step_trans = jnp.where(eye, 1.0, 0.0) - moved[:, :dk]
            step_add = moved[:, dk:]
            scores = dot_bt(query, key) * rrow
            visible = iota((tok, BLK), 1) <= REFL * iota((tok, BLK), 0) + (REFL - 1)
            scores = jnp.where(visible, scores, 0.0)
            read = dot3(split(scores), split(wu))
            project = query.astype(F32) - read[:, :dk]
            base = read[:, dk:]
            rows = slice(c * tok, (c + 1) * tok)
            if c == 0:
                trans, add = step_trans, step_add
                reach_ref[h, rows, :] = project
                base_ref[h, rows, :] = base
            else:
                before = split(jnp.concatenate([trans, add], axis=1))
                gone = dot3(split(project), before)
                reach_ref[h, rows, :] = gone[:, :dk]
                base_ref[h, rows, :] = gone[:, dk:] + base
                after = dot3(split(step_trans), before)
                trans, add = after[:, :dk], after[:, dk:] + step_add
        pair_ref[h, :, :dk] = trans
        pair_ref[h, :, dk:] = add


def chain_kernel(
    seqs, segs, heads,
    pair_ref, init_ref, reach_ref, base_ref, gain_ref, out_ref,
    rx, prefix, total, zx, outgoing, incoming,
    state_ref, put_sem, got_sem, zput_sem, zgot_sem, sput_sem, sgot_sem,
):
    dk = init_ref.shape[1]
    dv = init_ref.shape[2]
    span = seqs // heads
    me = lax.axis_index("seq")
    seg = lax.axis_index("seg")
    owner = lax.rem(me, span) == 0
    mine = me // span

    barrier = pltpu.get_barrier_semaphore()
    for d in range(1, seqs):
        pl.semaphore_signal(
            barrier, inc=1,
            device_id={"seq": lax.rem(me + d, seqs), "seg": seg}, device_id_type=MESH,
        )
    for d in range(1, segs):
        pl.semaphore_signal(
            barrier, inc=1,
            device_id={"seq": me, "seg": lax.rem(seg + d, segs)}, device_id_type=MESH,
        )
    pl.semaphore_wait(barrier, seqs + segs - 2)

    def put(h):
        return pltpu.make_async_remote_copy(
            src_ref=pair_ref.at[h], dst_ref=rx.at[me],
            send_sem=put_sem.at[h], recv_sem=got_sem.at[me],
            device_id={"seq": h * span, "seg": seg}, device_id_type=MESH,
        )

    for h in range(heads):

        @pl.when(me != h * span)
        def _():
            put(h).start()

    def zput(g):
        return pltpu.make_async_remote_copy(
            src_ref=total, dst_ref=zx.at[seg],
            send_sem=zput_sem.at[g], recv_sem=zgot_sem.at[seg],
            device_id={"seq": me, "seg": g}, device_id_type=MESH,
        )

    def zgot(g):
        return pltpu.make_async_remote_copy(
            src_ref=total, dst_ref=zx.at[g],
            send_sem=zput_sem.at[g], recv_sem=zgot_sem.at[g],
            device_id={"seq": me, "seg": g}, device_id_type=MESH,
        )

    def got(s):
        return pltpu.make_async_remote_copy(
            src_ref=rx.at[s], dst_ref=rx.at[s],
            send_sem=put_sem.at[0], recv_sem=got_sem.at[s],
            device_id={"seq": s, "seg": seg}, device_id_type=MESH,
        )

    def sput(s):
        return pltpu.make_async_remote_copy(
            src_ref=outgoing.at[s], dst_ref=incoming.at[mine],
            send_sem=sput_sem.at[s], recv_sem=sgot_sem.at[mine],
            device_id={"seq": s, "seg": seg}, device_id_type=MESH,
        )

    def sgot(h):
        return pltpu.make_async_remote_copy(
            src_ref=outgoing.at[0], dst_ref=incoming.at[h],
            send_sem=sput_sem.at[0], recv_sem=sgot_sem.at[h],
            device_id={"seq": h * span, "seg": seg}, device_id_type=MESH,
        )

    @pl.when(owner)
    def _():
        total[:, :dk] = jnp.where(iota((dk, dk), 0) == iota((dk, dk), 1), 1.0, 0.0).astype(F32)
        total[:, dk:] = jnp.zeros((dk, dv), F32)
        rx[me] = pair_ref[mine]

        def one(s, _):
            @pl.when(s != me)
            def _():
                got(s).wait_recv()

            prefix[s] = total[...]
            after = dot3(split(rx[s, :, :dk]), split(total[...]))
            total[:, :dk] = after[:, :dk]
            total[:, dk:] = after[:, dk:] + rx[s, :, dk:]
            return 0

        lax.fori_loop(0, seqs, one, 0)
        for g in range(1, segs):

            @pl.when(seg < g)
            def _():
                zput(g).start()

        state_ref[...] = init_ref[mine]
        for g in range(segs - 1):

            @pl.when(g < seg)
            def _():
                zgot(g).wait_recv()
                state_ref[...] = (
                    dot3(split(zx[g, :, :dk]), split(state_ref[...])) + zx[g, :, dk:]
                )

        def give(s, _):
            ready = dot3(split(prefix[s, :, :dk]), split(state_ref[...])) + prefix[s, :, dk:]

            @pl.when(s != me)
            def _():
                outgoing[s] = ready
                sput(s).start()

            @pl.when(s == me)
            def _():
                incoming[mine] = ready

            return 0

        lax.fori_loop(0, seqs, give, 0)

    for h in range(heads):

        @pl.when(me != h * span)
        def _():
            sgot(h).wait_recv()

        read = dot3(split(reach_ref[h]), split(incoming[h])) + base_ref[h]
        scale = lax.rsqrt(jnp.mean(read * read, axis=-1, keepdims=True) + 1e-6)
        normed = read * scale * gain_ref[h : h + 1, :]
        out_ref[:, h * dv : (h + 1) * dv] = normed.astype(BF16)

    for h in range(heads):

        @pl.when(me != h * span)
        def _():
            put(h).wait_send()

    @pl.when(owner)
    def _():
        for g in range(1, segs):

            @pl.when(seg < g)
            def _():
                zput(g).wait_send()

        def done(s, _):
            @pl.when(s != me)
            def _():
                sput(s).wait_send()

            return 0

        lax.fori_loop(0, seqs, done, 0)


def per_device(seqs, segs, query_rows, key_rows, value_rows, out_gain, initial_state):
    _, tokens, heads, dk = query_rows.shape
    dv = value_rows.shape[-1]
    steps = tokens * REFL
    query = query_rows.reshape(tokens, heads * dk)
    key = key_rows.reshape(steps, heads * dk)
    value = value_rows.reshape(steps, heads * dv)
    per = 2
    vmem = pl.BlockSpec(memory_space=pltpu.VMEM)
    count = per * (steps // BLK)
    pair, reach, base = pl.pallas_call(
        functools.partial(local_kernel, per),
        grid=(heads // per,),
        in_specs=[
            pl.BlockSpec((tokens, per * dk), lambda i: (0, i)),
            pl.BlockSpec((steps, per * dk), lambda i: (0, i)),
            pl.BlockSpec((steps, per * dv), lambda i: (0, i)),
        ],
        out_specs=[
            pl.BlockSpec((per, dk, dk + dv), lambda i: (i, 0, 0)),
            pl.BlockSpec((per, tokens, dk), lambda i: (i, 0, 0)),
            pl.BlockSpec((per, tokens, dv), lambda i: (i, 0, 0)),
        ],
        out_shape=[
            jax.ShapeDtypeStruct((heads, dk, dk + dv), F32),
            jax.ShapeDtypeStruct((heads, tokens, dk), F32),
            jax.ShapeDtypeStruct((heads, tokens, dv), F32),
        ],
        scratch_shapes=[
            pltpu.VMEM((count * SUB, BLK), F32),
            pltpu.VMEM((count * SUB, BLK), F32),
        ],
        name="local_part",
    )(query, key, value)
    wide = dk + dv
    out = pl.pallas_call(
        functools.partial(chain_kernel, seqs, segs, heads),
        in_specs=[vmem] * 5,
        out_specs=vmem,
        out_shape=jax.ShapeDtypeStruct((tokens, heads * dv), BF16),
        scratch_shapes=[
            pltpu.VMEM((seqs, dk, wide), F32),
            pltpu.VMEM((seqs, dk, wide), F32),
            pltpu.VMEM((dk, wide), F32),
            pltpu.VMEM((segs, dk, wide), F32),
            pltpu.VMEM((seqs, dk, dv), F32),
            pltpu.VMEM((heads, dk, dv), F32),
            pltpu.VMEM((dk, dv), F32),
            pltpu.SemaphoreType.DMA((heads,)),
            pltpu.SemaphoreType.DMA((seqs,)),
            pltpu.SemaphoreType.DMA((segs,)),
            pltpu.SemaphoreType.DMA((segs,)),
            pltpu.SemaphoreType.DMA((seqs,)),
            pltpu.SemaphoreType.DMA((heads,)),
        ],
        compiler_params=pltpu.CompilerParams(collective_id=0, has_side_effects=True),
        name="chain_part",
    )(pair, initial_state, reach, base, out_gain)
    return out.reshape(1, tokens, heads, dv)


def solution(mesh):
    return jax.shard_map(
        functools.partial(per_device, mesh.shape["seq"], mesh.shape["seg"]),
        mesh=mesh,
        in_specs=(
            P("seg", "seq", None, None),
            P("seg", "seq", None, None, None),
            P("seg", "seq", None, None, None),
            P(),
            P(),
        ),
        out_specs=P("seg", "seq", None, None),
        check_vma=False,
    )
```

time: 320 us -> 47.4 us (0.15)
  other arithmetic: 168 us -> 0 us
  waiting for transfers between devices: 72.6 us -> 0 us
  Pallas kernels: 0 us -> 41.5 us
  local copies, waits for them, and re-layouts: 36.5 us -> 5.63 us
  matrix products: 27.3 us -> 0 us
  between operations: 13.8 us -> 0.01 us
    another operation x7 -> x0, other arithmetic: 160 us -> none  [solve_single(): jax.scipy.linalg.solve_triangular(matrix, target, lower=True, unit_diagon...]
    all_gather x2 -> x0, waiting for transfers between devices: 72.6 us -> none  [the longest x1 37.8 us: per_device(): stacked = lax.all_gather(own_pair[None], 'seq', axis=0, tiled=True)]
    pallas_call x0 -> x2, Pallas kernels: none -> 41.5 us  [the longest x1 28.4 us: per_device(): pl.pallas_call(functools.partial(chain_kernel, seqs, segs, heads), in_spe...]
    dot_general x24 -> x0, matrix products: 24.1 us -> none  [the longest x13 9.22 us: compose(): jnp.einsum('...de,...ef->...df', second_trans, first_pair, precision=high...]
    squeeze x12 -> x0, local copies, waits for them, and re-layouts: 13.1 us -> none  [the longest x8 8.7 us: ordered_prefix(): closing, before_all = lax.scan(ordered_accumulate, identity_pair(), stacked)]
    dynamic_update_slice x10 -> x0, local copies, waits for them, and re-layouts: 8.53 us -> none  [the longest x8 6.85 us: ordered_prefix(): closing, before_all = lax.scan(ordered_accumulate, identity_pair(), stacked)]
    another operation x7 -> x0, local copies, waits for them, and re-layouts: 5.7 us -> none
    reshape x0 -> x2, local copies, waits for them, and re-layouts: none -> 3.87 us  [the longest x1 2.16 us: per_device(): value = value_rows.reshape(steps, heads * dv)]
  transfers between devices with their start and end apart: 2 -> 0, of which waited for: 2 -> 0; matrix products, arithmetic and copies ran while one was open for 2% -> 0% of each run, Pallas kernels for 0% -> 0%
where the time goes in v1:
time: 47.4 us; the launch traced here: 47.1 us
  Pallas kernels  41.5 us (88%)
  local copies, waits for them, and re-layouts  5.63 us (12%)
    pallas_call x1, Pallas kernels, per_device(): pl.pallas_call(functools.partial(chain_kernel, seqs, segs, heads), in_spe...  28.4 us
    pallas_call x1, Pallas kernels, per_device(): pl.pallas_call(functools.partial(local_kernel, per), grid=(heads // per,)...  13.1 us
    reshape x1, local copies, waits for them, and re-layouts, per_device(): value = value_rows.reshape(steps, heads * dv)  2.16 us
    unnamed x3, local copies, waits for them, and re-layouts  1.75 us
    reshape x1, local copies, waits for them, and re-layouts, per_device(): return out.reshape(1, tokens, heads, dv)  1.72 us

profile of v1, /device:TPU:29, one launch (start us, length us, event | category | flops | bytes accessed | tf_op | source)
XLA Modules:
  0.0 47.1 jit_solution(17629691545545579871)
XLA Ops:
  0.0 0.0 copy-start
  0.0 1.7 %copy.12 = bf16[32,8,4,128]{3,1,2,0:T(8,128)(2,1)} copy(bf16[32,8,4,128]{3,2,1,0:T(4,128)(2,1)} %bitcast.16) | data formatting | bytes 524288
  1.8 0.0 copy-done
  1.8 2.2 %copy_bitcast_fusion = (bf16[512,512]{1,0:T(8,128)(2,1)}, bf16[512,512]{1,0:T(8,128)(2,1)}) fusion(bf16[64,8,4,128]{3,2,1,0:T(4,128)(2,1)S(1)} %bitcast.14, bf16[64,8,4,128]{3,2,1,0:T(4,128)(2,1)} %bitcast.15), kind=kLoop, calls=%fused_computation | loop fusion | bytes 2097152 | tf_op jit(solution)/shard_map/reshape | solution.py:306
  3.9 13.1 %local_part.1 = (f32[4,128,256]{2,1,0:T(8,128)}, f32[4,256,128]{2,1,0:T(8,128)}, f32[4,256,128]{2,1,0:T(8,128)}) custom-call(bf16[256,512]{1,0:T(8,128)(2,1)} %bitcast.13, bf16[512,512]{1,0:T(8,128)(2,1)} %get-tuple-element.12.k_ref, bf16[512,512]{1,0:T(8,128)(2,1)} %get-tuple-element.11.v_ref), custom_call_target="tpu_custom_call" | custom-call | tf_op jit(solution)/shard_map/local_part/pallas_call | solution.py:310
  17.0 28.4 %chain_part.1 = bf16[256,512]{1,0:T(8,128)(2,1)} custom-call(f32[4,128,256]{2,1,0:T(8,128)} %get-tuple-element.8.pair_ref, f32[4,128,128]{2,1,0:T(8,128)} %init_ref.1, f32[4,256,128]{2,1,0:T(8,128)} %get-tuple-element.9.reach_ref, f32[4,256,128]{2,1,0:T(8,128)} %get-tuple-element.10.base_ref, f32[4,128]{1,0:T(4,128)} %gain_ref.1), custom_call_target="tpu_custom_call" | custom-call | tf_op jit(solution)/shard_map/chain_part/pallas_call | solution.py:335
  45.4 1.7 %reshape.15 = bf16[1,256,4,128]{3,2,1,0:T(4,128)(2,1)} reshape(bf16[256,512]{1,0:T(8,128)(2,1)} %chain_part.1) | data formatting | bytes 524288 | tf_op jit(solution)/shard_map/reshape | solution.py:358
Async XLA Ops:
  0.0 1.8 %copy-start = (bf16[1,256,2,4,128]{4,3,2,1,0:T(4,128)(2,1)S(1)}, bf16[1,256,2,4,128]{4,3,2,1,0:T(4,128)(2,1)}, u32[]{:S(2)}) copy-start(bf16[1,256,2,4,128]{4,3,2,1,0:T(4,128)(2,1)} %param.7) | copy-start | bytes 1572868

commit v2 on v1

v2 whole, which is shorter than its diff:
```python
import functools

import jax
import jax.numpy as jnp
from jax import lax
from jax.experimental import pallas as pl
from jax.experimental.pallas import tpu as pltpu
from jax.sharding import PartitionSpec as P

F32 = jnp.float32
BF16 = jnp.bfloat16
REFL = 2
BLK = 128
SUB = 32
MESH = pl.DeviceIdType.MESH


def dot(a, b):
    return lax.dot_general(a, b, (((1,), (0,)), ((), ())), preferred_element_type=F32)


def dot_bt(a, b):
    return lax.dot_general(a, b, (((1,), (1,)), ((), ())), preferred_element_type=F32)


def dot_at(a, b):
    return lax.dot_general(a, b, (((0,), (0,)), ((), ())), preferred_element_type=F32)


def split(x):
    high = x.astype(BF16)
    return high, (x - high.astype(F32)).astype(BF16)


def dot3(a, b):
    ah, al = a
    bh, bl = b
    return dot(jnp.concatenate([ah, al], 1), jnp.concatenate([bh, bh], 0)) + dot(ah, bl)


def dot2(a, exact):
    return dot(jnp.concatenate(a, 1), jnp.concatenate([exact, exact], 0))


def iota(shape, axis):
    return lax.broadcasted_iota(jnp.int32, shape, axis)


def grouped(x, size, odd):
    return [x[g * size : (g + 1) * size] for g in range(odd, x.shape[0] // size, 2)]


def factors(first, per, heads, nblk, kf, vf, dsc, nsc, kb, scaled_hi, scaled_lo, before, pair):
    dk = kf.shape[1]
    row, col = iota((BLK, BLK), 0), iota((BLK, BLK), 1)
    eye = row == col
    lane = iota((SUB, BLK), 1)
    count = per * nblk

    keys, lowers, rcols, rrows = [], [], [], []
    for n in range(count):
        h, c = n // nblk, n % nblk
        key = kf[pl.ds(c * BLK * heads + first + h, BLK, stride=heads), :].astype(BF16)
        kb[first + h, c] = key
        gram = dot_bt(key, key)
        diag = jnp.where(eye, gram, 0.0)
        rcol = lax.rsqrt(jnp.sum(diag, axis=1, keepdims=True) + 1e-6)
        rrow = lax.rsqrt(jnp.sum(diag, axis=0, keepdims=True) + 1e-6)
        lower = jnp.where(row > col, gram * (2.0 * rcol) * rrow, 0.0)
        packed = lower[:SUB]
        for g in range(1, BLK // SUB):
            packed = jnp.where(lane // SUB == g, lower[g * SUB : (g + 1) * SUB], packed)
        dsc[n * SUB : (n + 1) * SUB, :] = packed
        keys.append(key)
        lowers.append(lower)
        rcols.append(rcol)
        rrows.append(rrow)

    lane_c = iota((count, BLK), 1)
    solved = []
    for i in range(SUB):
        line = dsc[pl.ds(i, count, stride=SUB), :]
        total = jnp.where(lane_c % SUB == i, 1.0, 0.0)
        for j in range(i):
            factor = jnp.take_along_axis(line, (lane_c // SUB) * SUB + j, axis=1)
            total = total - factor * solved[j]
        solved.append(total)
        nsc[pl.ds(i, count, stride=SUB), :] = total

    inverses = []
    for n in range(count):
        packed = nsc[n * SUB : (n + 1) * SUB, :]
        inverses.append(
            jnp.concatenate(
                [jnp.where(lane // SUB == g, packed, 0.0) for g in range(BLK // SUB)], axis=0
            )
        )
    half = BLK // 2
    size = SUB
    while size < BLK:
        paired = iota((half, BLK), 1) // size == 2 * (iota((half, BLK), 0) // size)
        for n in range(count):
            inv = split(inverses[n])
            odd = jnp.concatenate(grouped(lowers[n], size, 1), 0)
            part = dot3(split(jnp.where(paired, odd, 0.0)), inv)
            blank = jnp.zeros((size, BLK), F32)
            spread = []
            for g in range(half // size):
                spread += [blank, part[g * size : (g + 1) * size]]
            own = tuple(jnp.concatenate(grouped(x, size, 1), 0) for x in inv)
            fill = dot3(own, split(jnp.concatenate(spread, 0)))
            even, odd = grouped(inverses[n], size, 0), grouped(inverses[n], size, 1)
            rows = []
            for g in range(half // size):
                rows += [even[g], odd[g] - fill[g * size : (g + 1) * size]]
            inverses[n] = jnp.concatenate(rows, 0)
        size *= 2

    for h in range(per):
        trans = add = None
        for c in range(nblk):
            n = h * nblk + c
            key, rcol, rrow = keys[n], rcols[n], rrows[n]
            value = vf[pl.ds(c * BLK * heads + first + h, BLK, stride=heads), :].astype(BF16)
            weights = dot2(split(inverses[n] * (2.0 * rrow)), key)
            updates = dot2(split(inverses[n] * 2.0), value)
            scaled = split(jnp.concatenate([weights, updates], axis=1) * rcol)
            scaled_hi[first + h, c] = scaled[0]
            scaled_lo[first + h, c] = scaled[1]
            moved = dot_at(jnp.concatenate([key, key], 0), jnp.concatenate(scaled, 0))
            step_trans = jnp.where(eye, 1.0, 0.0) - moved[:, :dk]
            step_add = moved[:, dk:]
            if c == 0:
                trans, add = step_trans, step_add
            else:
                so_far = jnp.concatenate([trans, add], axis=1)
                before[first + h, c] = so_far
                after = dot3(split(step_trans), split(so_far))
                trans, add = after[:, :dk], after[:, dk:] + step_add
        pair[first + h, :, :dk] = trans
        pair[first + h, :, dk:] = add


def readers(h, heads, nblk, qf, kb, scaled_hi, scaled_lo, before, reach, base):
    dk = qf.shape[1]
    tok = BLK // REFL
    visible = iota((tok, BLK), 1) <= REFL * iota((tok, BLK), 0) + (REFL - 1)
    for c in range(nblk):
        query = qf[pl.ds(c * tok * heads + h, tok, stride=heads), :]
        scores = jnp.where(visible, dot_bt(query.astype(BF16), kb[h, c]), 0.0)
        read = dot3(split(scores), (scaled_hi[h, c], scaled_lo[h, c]))
        project = query - read[:, :dk]
        local = read[:, dk:]
        rows = slice(c * tok, (c + 1) * tok)
        if c == 0:
            reach[h, rows, :] = project
            base[h, rows, :] = local
        else:
            gone = dot3(split(project), split(before[h, c]))
            reach[h, rows, :] = gone[:, :dk]
            base[h, rows, :] = gone[:, dk:] + local


def kernel(
    seqs, segs, heads, per,
    q_ref, k_ref, v_ref, gain_ref, init_ref, out_ref,
    qf, kf, vf, dsc, nsc, kb, scaled_hi, scaled_lo, before, pair, reach, base,
    rx, prefix, own_prefix, total, zx, first_state, zstate, own_state, state,
    put_sem, got_sem, zput_sem, zgot_sem, pput_sem, pgot_sem, sput_sem, sgot_sem,
):
    dk = init_ref.shape[1]
    dv = init_ref.shape[2]
    nblk = k_ref.shape[0] // (heads * BLK)
    span = seqs // heads
    me = lax.axis_index("seq")
    seg = lax.axis_index("seg")
    owner = lax.rem(me, span) == 0
    mine = me // span

    barrier = pltpu.get_barrier_semaphore()
    for d in range(1, seqs):
        pl.semaphore_signal(
            barrier, inc=1,
            device_id={"seq": lax.rem(me + d, seqs), "seg": seg}, device_id_type=MESH,
        )
    for d in range(1, segs):
        pl.semaphore_signal(
            barrier, inc=1,
            device_id={"seq": me, "seg": lax.rem(seg + d, segs)}, device_id_type=MESH,
        )

    def copy(src, dst, put, got, to_seq, to_seg):
        return pltpu.make_async_remote_copy(
            src_ref=src, dst_ref=dst, send_sem=put, recv_sem=got,
            device_id={"seq": to_seq, "seg": to_seg}, device_id_type=MESH,
        )

    def put(h):
        return copy(pair.at[h], rx.at[me], put_sem.at[h], got_sem.at[me], h * span, seg)

    def got(s):
        return copy(rx.at[s], rx.at[s], put_sem.at[0], got_sem.at[s], s, seg)

    def pput(s):
        return copy(prefix.at[s], own_prefix.at[mine], pput_sem.at[s], pgot_sem.at[mine], s, seg)

    def pgot(h):
        return copy(prefix.at[0], own_prefix.at[h], pput_sem.at[0], pgot_sem.at[h], h * span, seg)

    def sput(s):
        return copy(state, own_state.at[mine], sput_sem.at[s], sgot_sem.at[mine], s, seg)

    def sgot(h):
        return copy(state, own_state.at[h], sput_sem.at[0], sgot_sem.at[h], h * span, seg)

    def zput(g):
        return copy(total, zx.at[seg], zput_sem.at[g], zgot_sem.at[seg], me, g)

    def zgot(g):
        return copy(total, zx.at[g], zput_sem.at[g], zgot_sem.at[g], me, g)

    def fput(g):
        return copy(first_state, zstate, zput_sem.at[g], zgot_sem.at[0], me, g)

    kf[...] = k_ref[...].astype(F32)
    vf[...] = v_ref[...].astype(F32)
    qf[...] = q_ref[...].astype(F32)

    def local(i, _):
        factors(i * per, per, heads, nblk, kf, vf, dsc, nsc, kb, scaled_hi, scaled_lo, before, pair)

        @pl.when(i == 0)
        def _():
            pl.semaphore_wait(barrier, seqs + segs - 2)

        for d in range(per):
            h = i * per + d

            @pl.when(me != h * span)
            def _():
                put(h).start()

        return 0

    lax.fori_loop(0, heads // per, local, 0)

    def reading(h, _):
        readers(h, heads, nblk, qf, kb, scaled_hi, scaled_lo, before, reach, base)
        return 0

    lax.fori_loop(0, heads, reading, 0)

    @pl.when(owner)
    def _():
        total[:, :dk] = jnp.where(iota((dk, dk), 0) == iota((dk, dk), 1), 1.0, 0.0).astype(F32)
        total[:, dk:] = jnp.zeros((dk, dv), F32)
        rx[me] = pair[mine]

        def one(s, _):
            @pl.when(s != me)
            def _():
                got(s).wait_recv()

            so_far = total[...]
            prefix[s] = so_far

            @pl.when(s != me)
            def _():
                pput(s).start()

            @pl.when(s == me)
            def _():
                own_prefix[mine] = so_far

            after = dot3(split(rx[s, :, :dk]), split(so_far))
            total[:, :dk] = after[:, :dk]
            total[:, dk:] = after[:, dk:] + rx[s, :, dk:]
            return 0

        lax.fori_loop(0, seqs, one, 0)

        @pl.when(seg == 0)
        def _():
            first_state[...] = dot3(split(total[:, :dk]), split(init_ref[mine])) + total[:, dk:]
            for g in range(1, segs):
                fput(g).start()

        for g in range(2, segs):

            @pl.when((seg > 0) & (seg < g))
            def _():
                zput(g).start()

    def joining(h, _):
        @pl.when(me != h * span)
        def _():
            pgot(h).wait_recv()

        gone = dot3(split(reach[h]), split(own_prefix[h]))
        reach[h] = gone[:, :dk]
        base[h] = gone[:, dk:] + base[h]
        return 0

    lax.fori_loop(0, heads, joining, 0)

    @pl.when(owner)
    def _():
        @pl.when(seg == 0)
        def _():
            state[...] = init_ref[mine]

        @pl.when(seg > 0)
        def _():
            fput(0).wait_recv()
            state[...] = zstate[...]

        for g in range(1, segs - 1):

            @pl.when(g < seg)
            def _():
                zgot(g).wait_recv()
                state[...] = dot3(split(zx[g, :, :dk]), split(state[...])) + zx[g, :, dk:]

        def give(s, _):
            @pl.when(s != me)
            def _():
                sput(s).start()

            return 0

        lax.fori_loop(0, seqs, give, 0)
        own_state[mine] = state[...]

    for h in range(heads):

        @pl.when(me != h * span)
        def _():
            sgot(h).wait_recv()

        read = dot3(split(reach[h]), split(own_state[h])) + base[h]
        scale = lax.rsqrt(jnp.mean(read * read, axis=-1, keepdims=True) + 1e-6)
        normed = read * scale * gain_ref[h : h + 1, :]
        qf[pl.ds(h, read.shape[0], stride=heads), :] = normed
    out_ref[...] = qf[...].astype(BF16)

    for h in range(heads):

        @pl.when(me != h * span)
        def _():
            put(h).wait_send()

    @pl.when(owner)
    def _():
        @pl.when(seg == 0)
        def _():
            for g in range(1, segs):
                fput(g).wait_send()

        for g in range(2, segs):

            @pl.when((seg > 0) & (seg < g))
            def _():
                zput(g).wait_send()

        def done(s, _):
            @pl.when(s != me)
            def _():
                pput(s).wait_send()
                sput(s).wait_send()

            return 0

        lax.fori_loop(0, seqs, done, 0)


def per_device(seqs, segs, query_rows, key_rows, value_rows, out_gain, initial_state):
    _, tokens, heads, dk = query_rows.shape
    dv = value_rows.shape[-1]
    steps = tokens * REFL
    nblk = steps // BLK
    per = 2
    count = per * nblk
    wide = dk + dv
    vmem = pl.BlockSpec(memory_space=pltpu.VMEM)
    dma = pltpu.SemaphoreType.DMA
    out = pl.pallas_call(
        functools.partial(kernel, seqs, segs, heads, per),
        in_specs=[vmem] * 5,
        out_specs=vmem,
        out_shape=jax.ShapeDtypeStruct((tokens * heads, dv), BF16),
        scratch_shapes=[
            pltpu.VMEM((tokens * heads, dk), F32),
            pltpu.VMEM((steps * heads, dk), F32),
            pltpu.VMEM((steps * heads, dv), F32),
            pltpu.VMEM((count * SUB, BLK), F32),
            pltpu.VMEM((count * SUB, BLK), F32),
            pltpu.VMEM((heads, nblk, BLK, dk), BF16),
            pltpu.VMEM((heads, nblk, BLK, wide), BF16),
            pltpu.VMEM((heads, nblk, BLK, wide), BF16),
            pltpu.VMEM((heads, nblk, dk, wide), F32),
            pltpu.VMEM((heads, dk, wide), F32),
            pltpu.VMEM((heads, tokens, dk), F32),
            pltpu.VMEM((heads, tokens, dv), F32),
            pltpu.VMEM((seqs, dk, wide), F32),
            pltpu.VMEM((seqs, dk, wide), F32),
            pltpu.VMEM((heads, dk, wide), F32),
            pltpu.VMEM((dk, wide), F32),
            pltpu.VMEM((segs, dk, wide), F32),
            pltpu.VMEM((dk, dv), F32),
            pltpu.VMEM((dk, dv), F32),
            pltpu.VMEM((heads, dk, dv), F32),
            pltpu.VMEM((dk, dv), F32),
            dma((heads,)),
            dma((seqs,)),
            dma((segs,)),
            dma((segs,)),
            dma((seqs,)),
            dma((heads,)),
            dma((seqs,)),
            dma((heads,)),
        ],
        compiler_params=pltpu.CompilerParams(collective_id=0, has_side_effects=True),
        name="delta_product",
    )(
        query_rows.reshape(tokens * heads, dk),
        key_rows.reshape(steps * heads, dk),
        value_rows.reshape(steps * heads, dv),
        out_gain,
        initial_state,
    )
    return out.reshape(1, tokens, heads, dv)


def solution(mesh):
    return jax.shard_map(
        functools.partial(per_device, mesh.shape["seq"], mesh.shape["seg"]),
        mesh=mesh,
        in_specs=(
            P("seg", "seq", None, None),
            P("seg", "seq", None, None, None),
            P("seg", "seq", None, None, None),
            P(),
            P(),
        ),
        out_specs=P("seg", "seq", None, None),
        check_vma=False,
    )
```

time: 47.4 us -> 39.2 us (0.83)
  Pallas kernels: 41.5 us -> 37.3 us
  local copies, waits for them, and re-layouts: 5.63 us -> 1.74 us
    pallas_call x2 -> x1, Pallas kernels: 41.5 us -> 37.3 us  [per_device(): pl.pallas_call(functools.partial(kernel, seqs, segs, heads, per), in_spec...]
    reshape x2 -> x0, local copies, waits for them, and re-layouts: 3.87 us -> none  [the longest x1 2.16 us: per_device(): value = value_rows.reshape(steps, heads * dv)]
    unnamed x3 -> x1, local copies, waits for them, and re-layouts: 1.75 us -> 1.74 us
where the time goes in v2:
time: 39.2 us; the launch traced here: 39 us
  Pallas kernels  37.3 us (95%)
  local copies, waits for them, and re-layouts  1.74 us (4%)
    pallas_call x1, Pallas kernels, per_device(): pl.pallas_call(functools.partial(kernel, seqs, segs, heads, per), in_spec...  37.3 us
    unnamed x1, local copies, waits for them, and re-layouts  1.74 us

profile of v2, /device:TPU:29, one launch (start us, length us, event | category | flops | bytes accessed | tf_op | source)
XLA Modules:
  0.0 39.0 jit_solution(9378780709940919449)
XLA Ops:
  0.0 37.3 %delta_product.1 = bf16[1024,128]{1,0:T(8,128)(2,1)} custom-call(bf16[1024,128]{1,0:T(8,128)(2,1)} %bitcast.7, bf16[2048,128]{1,0:T(8,128)(2,1)} %bitcast.5, bf16[2048,128]{1,0:T(8,128)(2,1)} %bitcast.6, f32[4,128]{1,0:T(4,128)} %gain_ref.1, f32[4,128,128]{2,1,0:T(8,128)} %init_ref.1), custom_call_target="tpu_custom_call" | custom-call | tf_op jit(solution)/shard_map/delta_product/pallas_call | solution.py:386
  37.3 1.7 %copy.7 = bf16[1,256,4,128]{3,2,1,0:T(4,128)(2,1)} copy(bf16[1,256,4,128]{3,2,1,0:T(4,128)(2,1)} %bitcast.4) | data formatting | bytes 524288

commit v3 on v2

--- a/solution.py
+++ b/solution.py
@@ -11,7 +11,7 @@
 BF16 = jnp.bfloat16
 REFL = 2
 BLK = 128
-SUB = 32
+SUB = 16
 MESH = pl.DeviceIdType.MESH
 
 
@@ -165,8 +165,8 @@
     seqs, segs, heads, per,
     q_ref, k_ref, v_ref, gain_ref, init_ref, out_ref,
     qf, kf, vf, dsc, nsc, kb, scaled_hi, scaled_lo, before, pair, reach, base,
-    rx, prefix, own_prefix, total, zx, first_state, zstate, own_state, state,
-    put_sem, got_sem, zput_sem, zgot_sem, pput_sem, pgot_sem, sput_sem, sgot_sem,
+    rx, prefix, outgoing, total, zx, first_state, zstate, own_state, state,
+    put_sem, got_sem, zput_sem, zgot_sem, sput_sem, sgot_sem,
 ):
     dk = init_ref.shape[1]
     dv = init_ref.shape[2]
@@ -201,17 +201,11 @@
     def got(s):
         return copy(rx.at[s], rx.at[s], put_sem.at[0], got_sem.at[s], s, seg)
 
-    def pput(s):
-        return copy(prefix.at[s], own_prefix.at[mine], pput_sem.at[s], pgot_sem.at[mine], s, seg)
-
-    def pgot(h):
-        return copy(prefix.at[0], own_prefix.at[h], pput_sem.at[0], pgot_sem.at[h], h * span, seg)
-
     def sput(s):
-        return copy(state, own_state.at[mine], sput_sem.at[s], sgot_sem.at[mine], s, seg)
+        return copy(outgoing.at[s], own_state.at[mine], sput_sem.at[s], sgot_sem.at[mine], s, seg)
 
     def sgot(h):
-        return copy(state, own_state.at[h], sput_sem.at[0], sgot_sem.at[h], h * span, seg)
+        return copy(outgoing.at[0], own_state.at[h], sput_sem.at[0], sgot_sem.at[h], h * span, seg)
 
     def zput(g):
         return copy(total, zx.at[seg], zput_sem.at[g], zgot_sem.at[seg], me, g)
@@ -227,14 +221,15 @@
     qf[...] = q_ref[...].astype(F32)
 
     def local(i, _):
-        factors(i * per, per, heads, nblk, kf, vf, dsc, nsc, kb, scaled_hi, scaled_lo, before, pair)
+        turn = lax.rem(i + 1 + mine // per, heads // per)
+        factors(turn * per, per, heads, nblk, kf, vf, dsc, nsc, kb, scaled_hi, scaled_lo, before, pair)
 
         @pl.when(i == 0)
         def _():
             pl.semaphore_wait(barrier, seqs + segs - 2)
 
         for d in range(per):
-            h = i * per + d
+            h = turn * per + d
 
             @pl.when(me != h * span)
             def _():
@@ -263,15 +258,6 @@
 
             so_far = total[...]
             prefix[s] = so_far
-
-            @pl.when(s != me)
-            def _():
-                pput(s).start()
-
-            @pl.when(s == me)
-            def _():
-                own_prefix[mine] = so_far
-
             after = dot3(split(rx[s, :, :dk]), split(so_far))
             total[:, :dk] = after[:, :dk]
             total[:, dk:] = after[:, dk:] + rx[s, :, dk:]
@@ -291,18 +277,6 @@
             def _():
                 zput(g).start()
 
-    def joining(h, _):
-        @pl.when(me != h * span)
-        def _():
-            pgot(h).wait_recv()
-
-        gone = dot3(split(reach[h]), split(own_prefix[h]))
-        reach[h] = gone[:, :dk]
-        base[h] = gone[:, dk:] + base[h]
-        return 0
-
-    lax.fori_loop(0, heads, joining, 0)
-
     @pl.when(owner)
     def _():
         @pl.when(seg == 0)
@@ -322,14 +296,20 @@
                 state[...] = dot3(split(zx[g, :, :dk]), split(state[...])) + zx[g, :, dk:]
 
         def give(s, _):
+            ready = dot3(split(prefix[s, :, :dk]), split(state[...])) + prefix[s, :, dk:]
+
             @pl.when(s != me)
             def _():
+                outgoing[s] = ready
                 sput(s).start()
 
+            @pl.when(s == me)
+            def _():
+                own_state[mine] = ready
+
             return 0
 
         lax.fori_loop(0, seqs, give, 0)
-        own_state[mine] = state[...]
 
     for h in range(heads):
 
@@ -365,7 +345,6 @@
         def done(s, _):
             @pl.when(s != me)
             def _():
-                pput(s).wait_send()
                 sput(s).wait_send()
 
             return 0
@@ -403,7 +382,7 @@
             pltpu.VMEM((heads, tokens, dv), F32),
             pltpu.VMEM((seqs, dk, wide), F32),
             pltpu.VMEM((seqs, dk, wide), F32),
-            pltpu.VMEM((heads, dk, wide), F32),
+            pltpu.VMEM((seqs, dk, dv), F32),
             pltpu.VMEM((dk, wide), F32),
             pltpu.VMEM((segs, dk, wide), F32),
             pltpu.VMEM((dk, dv), F32),
@@ -414,8 +393,6 @@
             dma((seqs,)),
             dma((segs,)),
             dma((segs,)),
-            dma((seqs,)),
-            dma((heads,)),
             dma((seqs,)),
             dma((heads,)),
         ],

time: 39.2 us -> 37.8 us (0.964)
  Pallas kernels: 37.3 us -> 35.8 us
    pallas_call x1, Pallas kernels: 37.3 us -> 35.8 us  [per_device(): pl.pallas_call(functools.partial(kernel, seqs, segs, heads, per), in_spec...]
where the time goes in v3:
time: 37.8 us; the launch traced here: 37.6 us
  Pallas kernels  35.8 us (95%)
  local copies, waits for them, and re-layouts  1.74 us (5%)
    pallas_call x1, Pallas kernels, per_device(): pl.pallas_call(functools.partial(kernel, seqs, segs, heads, per), in_spec...  35.8 us
    unnamed x1, local copies, waits for them, and re-layouts  1.74 us

profile of v3, /device:TPU:29, one launch (start us, length us, event | category | flops | bytes accessed | tf_op | source)
XLA Modules:
  0.0 37.6 jit_solution(15049207342943327597)
XLA Ops:
  0.0 35.8 %delta_product.1 = bf16[1024,128]{1,0:T(8,128)(2,1)} custom-call(bf16[1024,128]{1,0:T(8,128)(2,1)} %bitcast.7, bf16[2048,128]{1,0:T(8,128)(2,1)} %bitcast.5, bf16[2048,128]{1,0:T(8,128)(2,1)} %bitcast.6, f32[4,128]{1,0:T(4,128)} %gain_ref.1, f32[4,128,128]{2,1,0:T(8,128)} %init_ref.1), custom_call_target="tpu_custom_call" | custom-call | tf_op jit(solution)/shard_map/delta_product/pallas_call | solution.py:365
  35.9 1.7 %copy.7 = bf16[1,256,4,128]{3,2,1,0:T(4,128)(2,1)} copy(bf16[1,256,4,128]{3,2,1,0:T(4,128)(2,1)} %bitcast.4) | data formatting | bytes 524288

commit v4 on v3

--- a/solution.py
+++ b/solution.py
@@ -12,6 +12,7 @@
 REFL = 2
 BLK = 128
 SUB = 16
+LANES = 128
 MESH = pl.DeviceIdType.MESH
 
 
@@ -35,11 +36,19 @@
 def dot3(a, b):
     ah, al = a
     bh, bl = b
-    return dot(jnp.concatenate([ah, al], 1), jnp.concatenate([bh, bh], 0)) + dot(ah, bl)
+    rows, width = ah.shape[0], bh.shape[1]
+    both = jnp.concatenate([ah, al], 0)
+    if width <= LANES:
+        full = dot(both, jnp.concatenate([bh, bl], 1))
+        return full[:rows, :width] + (full[:rows, width:] + full[rows:, :width])
+    full = dot(both, bh)
+    return full[:rows] + (full[rows:] + dot(ah, bl))
 
 
 def dot2(a, exact):
-    return dot(jnp.concatenate(a, 1), jnp.concatenate([exact, exact], 0))
+    rows = a[0].shape[0]
+    full = dot(jnp.concatenate(a, 0), exact)
+    return full[:rows] + full[rows:]
 
 
 def iota(shape, axis):
@@ -127,7 +136,7 @@
             scaled = split(jnp.concatenate([weights, updates], axis=1) * rcol)
             scaled_hi[first + h, c] = scaled[0]
             scaled_lo[first + h, c] = scaled[1]
-            moved = dot_at(jnp.concatenate([key, key], 0), jnp.concatenate(scaled, 0))
+            moved = dot_at(key, scaled[0]) + dot_at(key, scaled[1])
             step_trans = jnp.where(eye, 1.0, 0.0) - moved[:, :dk]
             step_add = moved[:, dk:]
             if c == 0:
@@ -165,7 +174,7 @@
     seqs, segs, heads, per,
     q_ref, k_ref, v_ref, gain_ref, init_ref, out_ref,
     qf, kf, vf, dsc, nsc, kb, scaled_hi, scaled_lo, before, pair, reach, base,
-    rx, prefix, outgoing, total, zx, first_state, zstate, own_state, state,
+    rx, prefix, outgoing, total, tree, zx, first_state, zstate, own_state, state,
     put_sem, got_sem, zput_sem, zgot_sem, sput_sem, sgot_sem,
 ):
     dk = init_ref.shape[1]
@@ -208,10 +217,10 @@
         return copy(outgoing.at[0], own_state.at[h], sput_sem.at[0], sgot_sem.at[h], h * span, seg)
 
     def zput(g):
-        return copy(total, zx.at[seg], zput_sem.at[g], zgot_sem.at[seg], me, g)
+        return copy(tree.at[seqs - 2], zx.at[seg], zput_sem.at[g], zgot_sem.at[seg], me, g)
 
     def zgot(g):
-        return copy(total, zx.at[g], zput_sem.at[g], zgot_sem.at[g], me, g)
+        return copy(tree.at[seqs - 2], zx.at[g], zput_sem.at[g], zgot_sem.at[g], me, g)
 
     def fput(g):
         return copy(first_state, zstate, zput_sem.at[g], zgot_sem.at[0], me, g)
@@ -251,11 +260,40 @@
         total[:, dk:] = jnp.zeros((dk, dv), F32)
         rx[me] = pair[mine]
 
+        def arrived(s, _):
+            @pl.when(s != me)
+            def _():
+                got(s).wait_recv()
+
+            return 0
+
+        lax.fori_loop(0, seqs, arrived, 0)
+        parts = [rx.at[s] for s in range(seqs)]
+        slot = 0
+        while len(parts) > 1:
+            joined = []
+            for early, late in zip(parts[::2], parts[1::2]):
+                after = dot3(split(late[:, :dk]), split(early[...]))
+                tree[slot, :, :dk] = after[:, :dk]
+                tree[slot, :, dk:] = after[:, dk:] + late[:, dk:]
+                joined.append(tree.at[slot])
+                slot += 1
+            parts = joined + (parts[-1:] if len(parts) % 2 else [])
+
+        @pl.when(seg == 0)
+        def _():
+            whole = tree[seqs - 2]
+            first_state[...] = dot3(split(whole[:, :dk]), split(init_ref[mine])) + whole[:, dk:]
+            for g in range(1, segs):
+                fput(g).start()
+
+        for g in range(2, segs):
+
+            @pl.when((seg > 0) & (seg < g))
+            def _():
+                zput(g).start()
+
         def one(s, _):
-            @pl.when(s != me)
-            def _():
-                got(s).wait_recv()
-
             so_far = total[...]
             prefix[s] = so_far
             after = dot3(split(rx[s, :, :dk]), split(so_far))
@@ -265,18 +303,6 @@
 
         lax.fori_loop(0, seqs, one, 0)
 
-        @pl.when(seg == 0)
-        def _():
-            first_state[...] = dot3(split(total[:, :dk]), split(init_ref[mine])) + total[:, dk:]
-            for g in range(1, segs):
-                fput(g).start()
-
-        for g in range(2, segs):
-
-            @pl.when((seg > 0) & (seg < g))
-            def _():
-                zput(g).start()
-
     @pl.when(owner)
     def _():
         @pl.when(seg == 0)
@@ -295,7 +321,8 @@
                 zgot(g).wait_recv()
                 state[...] = dot3(split(zx[g, :, :dk]), split(state[...])) + zx[g, :, dk:]
 
-        def give(s, _):
+        def give(k, _):
+            s = lax.rem(2 * seqs - 2 - me + k, seqs)
             ready = dot3(split(prefix[s, :, :dk]), split(state[...])) + prefix[s, :, dk:]
 
             @pl.when(s != me)
@@ -384,6 +411,7 @@
             pltpu.VMEM((seqs, dk, wide), F32),
             pltpu.VMEM((seqs, dk, dv), F32),
             pltpu.VMEM((dk, wide), F32),
+            pltpu.VMEM((seqs - 1, dk, wide), F32),
             pltpu.VMEM((segs, dk, wide), F32),
             pltpu.VMEM((dk, dv), F32),
             pltpu.VMEM((dk, dv), F32),

time: 37.8 us -> 31.2 us (0.83)
  Pallas kernels: 35.8 us -> 29 us
    pallas_call x1, Pallas kernels: 35.8 us -> 29 us  [per_device(): pl.pallas_call(functools.partial(kernel, seqs, segs, heads, per), in_spec...]
where the time goes in v4:
time: 31.2 us; the launch traced here: 30.8 us
  Pallas kernels  29 us (93%)
  local copies, waits for them, and re-layouts  1.74 us (6%)
    pallas_call x1, Pallas kernels, per_device(): pl.pallas_call(functools.partial(kernel, seqs, segs, heads, per), in_spec...  29 us
    unnamed x1, local copies, waits for them, and re-layouts  1.74 us

profile of v4, /device:TPU:29, one launch (start us, length us, event | category | flops | bytes accessed | tf_op | source)
XLA Modules:
  0.0 30.8 jit_solution(18433189318244627692)
XLA Ops:
  0.0 29.0 %delta_product.1 = bf16[1024,128]{1,0:T(8,128)(2,1)} custom-call(bf16[1024,128]{1,0:T(8,128)(2,1)} %bitcast.7, bf16[2048,128]{1,0:T(8,128)(2,1)} %bitcast.5, bf16[2048,128]{1,0:T(8,128)(2,1)} %bitcast.6, f32[4,128]{1,0:T(4,128)} %gain_ref.1, f32[4,128,128]{2,1,0:T(8,128)} %init_ref.1), custom_call_target="tpu_custom_call" | custom-call | tf_op jit(solution)/shard_map/delta_product/pallas_call | solution.py:392
  29.1 1.7 %copy.7 = bf16[1,256,4,128]{3,2,1,0:T(4,128)(2,1)} copy(bf16[1,256,4,128]{3,2,1,0:T(4,128)(2,1)} %bitcast.4) | data formatting | bytes 524288

commit v5 on v4

--- a/solution.py
+++ b/solution.py
@@ -231,6 +231,10 @@
 
     def local(i, _):
         turn = lax.rem(i + 1 + mine // per, heads // per)
+        if heads == 4 and per == 1:
+            left = heads - 1 - i
+            row, col = lax.rem(mine // 2 + left // 2, 2), lax.rem(mine + left, 2)
+            turn = 2 * row + col
         factors(turn * per, per, heads, nblk, kf, vf, dsc, nsc, kb, scaled_hi, scaled_lo, before, pair)
 
         @pl.when(i == 0)
@@ -384,7 +388,7 @@
     dv = value_rows.shape[-1]
     steps = tokens * REFL
     nblk = steps // BLK
-    per = 2
+    per = 1
     count = per * nblk
     wide = dk + dv
     vmem = pl.BlockSpec(memory_space=pltpu.VMEM)

time: 31.2 us -> 34.9 us (1.12)
  Pallas kernels: 29 us -> 32.7 us
    pallas_call x1, Pallas kernels: 29 us -> 32.7 us  [per_device(): pl.pallas_call(functools.partial(kernel, seqs, segs, heads, per), in_spec...]
where the time goes in v5:
time: 34.9 us; the launch traced here: 34.4 us
  Pallas kernels  32.7 us (94%)
  local copies, waits for them, and re-layouts  1.74 us (5%)
    pallas_call x1, Pallas kernels, per_device(): pl.pallas_call(functools.partial(kernel, seqs, segs, heads, per), in_spec...  32.7 us
    unnamed x1, local copies, waits for them, and re-layouts  1.74 us

profile of v5, /device:TPU:29, one launch (start us, length us, event | category | flops | bytes accessed | tf_op | source)
XLA Modules:
  0.0 34.4 jit_solution(12456762501027736882)
XLA Ops:
  0.0 32.7 %delta_product.1 = bf16[1024,128]{1,0:T(8,128)(2,1)} custom-call(bf16[1024,128]{1,0:T(8,128)(2,1)} %bitcast.7, bf16[2048,128]{1,0:T(8,128)(2,1)} %bitcast.5, bf16[2048,128]{1,0:T(8,128)(2,1)} %bitcast.6, f32[4,128]{1,0:T(4,128)} %gain_ref.1, f32[4,128,128]{2,1,0:T(8,128)} %init_ref.1), custom_call_target="tpu_custom_call" | custom-call | tf_op jit(solution)/shard_map/delta_product/pallas_call | solution.py:396
  32.7 1.7 %copy.7 = bf16[1,256,4,128]{3,2,1,0:T(4,128)(2,1)} copy(bf16[1,256,4,128]{3,2,1,0:T(4,128)(2,1)} %bitcast.4) | data formatting | bytes 524288
